TPU v7x, 32 devices: a whole 2x2x4 slice. The times are simulated.
32 devices in a mesh: img: 16 (over z, x, core), row: 2 (over y).
Axes of the slice: x: 2, y: 2, z: 4, core: 2. Of those that a mesh axis runs over, the one named last changes fastest.
Arguments:
- llm_hidden: bfloat16 [8192, 6656], P('img', 'row'), may hold values from -96 to 96
- slot_start: int32 [16], P('img'), may hold values from 0 to 448
- image_group: int32 [16], replicated, may hold values from 0 to 15, each once
- timesteps: int32 [16], P('img'), may hold values from 0 to 999
- latents: float32 [16, 4, 16, 128], P('img', None, 'row'), may hold values from -6 to 6
- noise: float32 [16, 4, 16, 128], P('img', None, 'row'), may hold values from -6 to 6
- kv_weight: bfloat16 [6656, 640], P('row'), may hold values from -0.078125 to 0.078125
- in_weight: bfloat16 [3, 3, 320, 4], replicated, may hold values from -1 to 1
- res_weight: bfloat16 [3, 3, 320, 320], replicated, may hold values from -0.109375 to 0.109375
- query_weight: bfloat16 [320, 320], replicated, may hold values from -0.3125 to 0.3125
- out_weight: bfloat16 [320, 320], replicated, may hold values from -0.3125 to 0.3125
- cotangent: bfloat16 [16, 320, 16, 128], P('img', None, 'row'), may hold values from -6 to 6
Outputs:
- block_out: bfloat16 [16, 320, 16, 128], P('img', None, 'row')
- grad_hidden: bfloat16 [8192, 6656], P('img', 'row')
- grad_kv_weight: bfloat16 [6656, 640], P('row')
- grad_res_weight: bfloat16 [3, 3, 320, 320], replicated
- grad_query_weight: bfloat16 [320, 320], replicated
- grad_out_weight: bfloat16 [320, 320], replicated
Inputs may be any that keep to these rules, and one draw needn't show every extreme that they name: `slot_start`: each image's 64 condition rows lie inside its own sequence of 512 tokens. `image_group`: every group denoises exactly one image.
All inputs are finite; a program needn't handle non-finite values.
Results may differ from a plain program's by a relative error of at most 0.035.
The roundings to bfloat16 on the way count: a program that leaves them out, or rounds other values in their place, can miss the bound.
Values may be sent and summed in bfloat16 or wider, within the bound.
No kernel may reach another device: no remote copies, remote signals or barrier semaphores. Data moves between devices by JAX's collectives and lax.ppermute only.
A program may use at most 128 MiB of HBM per device.

v0:
```python
import math
import jax
import jax.numpy as jnp
from jax import lax
from jax.sharding import PartitionSpec as P

HEAD_DIM = 64
SLOTS = 64


def extended(cells, sides, width):
    for axis, dim in sides:
        count = lax.axis_size(axis)
        ends = count - 1
        head = lax.slice_in_dim(cells, 0, width, axis=dim)
        tail = lax.slice_in_dim(cells, cells.shape[dim] - width, cells.shape[dim], axis=dim)
        cells = jnp.concatenate(
            [
                lax.ppermute(tail, axis, [(i, (i + 1) % count) for i in range(ends)]),
                cells,
                lax.ppermute(head, axis, [((i + 1) % count, i) for i in range(ends)]),
            ],
            axis=dim,
        )
    return cells


def weighted_product(form, left, right):
    return jnp.einsum(form, left, right, preferred_element_type=jnp.float32)


def noise_levels():
    plan = jnp.linspace(0.00085**0.5, 0.012**0.5, 1000, dtype=jnp.float32) ** 2
    return jnp.exp(jnp.cumsum(jnp.log(1.0 - plan)))


def noisy_input(latent, noise_one, timestep):
    levels = noise_levels()
    picked = jnp.sum(jnp.where(jnp.arange(levels.shape[0]) == timestep, levels, 0.0))
    return (jnp.sqrt(picked) * latent + jnp.sqrt(1.0 - picked) * noise_one).astype(jnp.bfloat16)


def time_shift(timestep, channel_total):
    half_count = channel_total // 2
    frequency = jnp.exp(-math.log(10000.0) * jnp.arange(half_count, dtype=jnp.float32) / half_count)
    angles = timestep.astype(jnp.float32) * frequency
    return jnp.concatenate([jnp.cos(angles), jnp.sin(angles)])


def pad_columns(field):
    return jnp.pad(field, ((0, 0), (0, 0), (1, 1)))


def convolve(padded, weight, row_count, col_count):
    running = jnp.zeros((weight.shape[2], row_count * col_count), jnp.float32)
    for row_tap in range(3):
        for col_tap in range(3):
            window = padded[
                :, row_tap : row_tap + row_count, col_tap : col_tap + col_count
            ].reshape(padded.shape[0], row_count * col_count)
            running = running + jnp.dot(
                weight[row_tap, col_tap], window, preferred_element_type=jnp.float32
            )
    return running


def filter_grad(padded, upstream, row_count, col_count):
    tap_list = []
    for row_tap in range(3):
        for col_tap in range(3):
            window = padded[
                :, row_tap : row_tap + row_count, col_tap : col_tap + col_count
            ].reshape(padded.shape[0], row_count * col_count)
            tap_list.append(
                lax.dot_general(
                    upstream, window, (((1,), (1,)), ((), ())), preferred_element_type=jnp.float32
                )
            )
    return jnp.stack(tap_list).reshape(3, 3, upstream.shape[0], padded.shape[0])


def block_pass(
    noisy, timestep, group_kv, upstream, in_weight, res_weight, query_weight, out_weight
):
    channel_total = in_weight.shape[2]
    row_count, col_count = (noisy.shape[1], noisy.shape[2])
    latent_cell_count = row_count * col_count
    condition_slot_count = group_kv.shape[0]
    head_count = channel_total // HEAD_DIM
    logit_scale = HEAD_DIM ** (-0.5)
    noisy_pad = pad_columns(extended(noisy, (("row", 1),), 1))
    first = convolve(noisy_pad, in_weight, row_count, col_count)
    hidden_act = jax.nn.silu(first + time_shift(timestep, channel_total)[:, None]).astype(
        jnp.bfloat16
    )
    act_pad = pad_columns(
        extended(hidden_act.reshape(channel_total, row_count, col_count), (("row", 1),), 1)
    )
    residual = (first + convolve(act_pad, res_weight, row_count, col_count)).astype(jnp.bfloat16)
    query = jnp.dot(query_weight, residual, preferred_element_type=jnp.float32).astype(jnp.bfloat16)
    query_per_head = query.reshape(head_count, HEAD_DIM, latent_cell_count)
    key_matrix = group_kv[:, :channel_total].reshape(condition_slot_count, head_count, HEAD_DIM)
    value_matrix = group_kv[:, channel_total:].reshape(condition_slot_count, head_count, HEAD_DIM)
    score_matrix = weighted_product("isf,tis->itf", query_per_head, key_matrix) * logit_scale
    softmax_full = jax.nn.softmax(score_matrix, axis=1)
    softmax_reduced_precision = softmax_full.astype(jnp.bfloat16)
    attention_output = (
        weighted_product("cuo,ucb->cbo", softmax_reduced_precision, value_matrix)
        .astype(jnp.bfloat16)
        .reshape(channel_total, latent_cell_count)
    )
    block_out = (
        residual.astype(jnp.float32)
        + jnp.dot(out_weight, attention_output, preferred_element_type=jnp.float32)
    ).astype(jnp.bfloat16)
    upstream = upstream.reshape(channel_total, latent_cell_count)
    out_grad = lax.dot_general(
        upstream, attention_output, (((1,), (1,)), ((), ())), preferred_element_type=jnp.float32
    )
    grad_att = lax.dot_general(
        out_weight, upstream, (((0,), (0,)), ((), ())), preferred_element_type=jnp.float32
    ).astype(jnp.bfloat16)
    head_gradient = grad_att.reshape(head_count, HEAD_DIM, latent_cell_count)
    probability_gradient = weighted_product("isf,tis->itf", head_gradient, value_matrix)
    score_gradient = (
        logit_scale
        * softmax_full
        * (
            probability_gradient
            - jnp.sum(softmax_full * probability_gradient, axis=1, keepdims=True)
        )
    ).astype(jnp.bfloat16)
    query_gradient = (
        weighted_product("cuo,ucb->cbo", score_gradient, key_matrix)
        .astype(jnp.bfloat16)
        .reshape(channel_total, latent_cell_count)
    )
    key_gradient = weighted_product("exv,ewv->xew", score_gradient, query_per_head).reshape(
        condition_slot_count, channel_total
    )
    value_gradient = weighted_product(
        "exv,ewv->xew", softmax_reduced_precision, head_gradient
    ).reshape(condition_slot_count, channel_total)
    grad_kv = jnp.concatenate([key_gradient, value_gradient], axis=1)
    query_grad = lax.dot_general(
        query_gradient, residual, (((1,), (1,)), ((), ())), preferred_element_type=jnp.float32
    )
    grad_resid = (
        upstream.astype(jnp.float32)
        + lax.dot_general(
            query_weight,
            query_gradient,
            (((0,), (0,)), ((), ())),
            preferred_element_type=jnp.float32,
        )
    ).astype(jnp.bfloat16)
    res_grad = filter_grad(act_pad, grad_resid, row_count, col_count)
    return (
        block_out.reshape(channel_total, row_count, col_count),
        grad_kv,
        res_grad,
        query_grad,
        out_grad,
    )


def shards(
    llm_hidden,
    slot_start,
    image_group,
    timesteps,
    latents,
    noise,
    kv_weight,
    in_weight,
    res_weight,
    query_weight,
    out_weight,
    cotangent,
):
    own_index = lax.axis_index("img")
    condition = lax.dynamic_slice_in_dim(llm_hidden, slot_start[0], SLOTS, 0)
    kv_part = jnp.dot(condition, kv_weight, preferred_element_type=jnp.float32)
    source_group = lax.dynamic_index_in_dim(image_group, own_index, 0, keepdims=False)
    kv_band = lax.psum_scatter(kv_part, "row", scatter_dimension=0, tiled=True).astype(jnp.bfloat16)
    selected = (image_group == own_index)[:, None, None]
    routed_band = jnp.sum(
        jnp.where(
            selected,
            lax.all_gather(kv_band[None], "img", axis=0, tiled=True).astype(jnp.float32),
            0.0,
        ),
        axis=0,
    ).astype(jnp.bfloat16)
    group_kv = lax.all_gather(routed_band, "row", axis=0, tiled=True)
    noisy = noisy_input(latents[0], noise[0], timesteps[0])
    block_out, grad_kv, res_grad, query_grad, out_grad = block_pass(
        noisy, timesteps[0], group_kv, cotangent[0], in_weight, res_weight, query_weight, out_weight
    )
    grad_band = lax.psum_scatter(
        grad_kv.astype(jnp.bfloat16), "row", scatter_dimension=0, tiled=True
    )
    shard_piece = lax.all_gather(grad_band[None], "img", axis=0, tiled=True)
    indices = jnp.arange(shard_piece.shape[0], dtype=jnp.int32)
    selected = (indices == source_group)[:, None, None]
    routed_grad = jnp.sum(jnp.where(selected, shard_piece.astype(jnp.float32), 0.0), axis=0).astype(
        jnp.bfloat16
    )
    grad_image = lax.all_gather(routed_grad, "row", axis=0, tiled=True)
    grad_condition = lax.dot_general(
        grad_image, kv_weight, (((1,), (1,)), ((), ())), preferred_element_type=jnp.float32
    ).astype(jnp.bfloat16)
    grad_hidden = lax.dynamic_update_slice_in_dim(
        jnp.zeros_like(llm_hidden), grad_condition, slot_start[0], 0
    )
    kv_weight_part = lax.dot_general(
        condition, grad_image, (((0,), (0,)), ((), ())), preferred_element_type=jnp.float32
    )
    kv_weight_total = lax.psum(kv_weight_part.astype(jnp.bfloat16), "img").astype(jnp.float32)
    grad_kv_weight = (kv_weight_total * (lax.axis_size("img") * SLOTS) ** (-0.5)).astype(
        jnp.bfloat16
    )
    weight_scale = (
        lax.axis_size("img") * lax.axis_size("row") * latents.shape[2] * latents.shape[3]
    ) ** (-0.5)
    res_total, query_total, out_total = lax.psum((res_grad, query_grad, out_grad), ("img", "row"))
    grad_res_weight = (res_total * weight_scale).astype(jnp.bfloat16)
    grad_query_weight = (query_total * weight_scale).astype(jnp.bfloat16)
    grad_out_weight = (out_total * weight_scale).astype(jnp.bfloat16)
    return (
        block_out[None],
        grad_hidden,
        grad_kv_weight,
        grad_res_weight,
        grad_query_weight,
        grad_out_weight,
    )


def solution(mesh):
    return jax.shard_map(
        shards,
        mesh=mesh,
        in_specs=(
            P("img", "row"),
            P("img"),
            P(),
            P("img"),
            P("img", None, "row", None),
            P("img", None, "row", None),
            P("row", None),
            P(),
            P(),
            P(),
            P(),
            P("img", None, "row", None),
        ),
        out_specs=(P("img", None, "row", None), P("img", "row"), P("row", None), P(), P(), P()),
        check_vma=False,
    )
```

profile of v0, /device:TPU:0, one launch (start us, length us, event | category | flops | bytes accessed | tf_op | source)
XLA Modules:
  0.0 399.7 jit_solution(4542939119349975653)
XLA Ops:
  8.8 0.6 select_reduce_fusion
  10.8 0.7 add_convert_fusion
  11.6 4.9 %collective-permute-start = (bf16[4,1,128]{2,1,0:T(2,128)(2,1)S(1)}, bf16[4,1,128]{2,1,0:T(2,128)(2,1)S(1)}, u32[]{:S(2)}, u32[]{:S(2)}) collective-permute-start(bf16[4,1,128]{2,1,0:T(2,128)(2,1)S(1)} %get-tuple-element.29), channel_id=1, source_target_pairs={{0,1},{2,3},{4,5},{6,7},{8,9},{10,11},{12,13},{14,15},{16,17},{18,... | collective-permute-start | bytes 3080 | tf_op jit(solution)/shard_map/ppermute | solution.py:19
  16.5 1.3 collective-permute-start.1
  18.5 3.7 fusion.68
  22.3 2.6 convolution_convert_fusion.4
  28.2 0.6 fusion.19
  29.2 4.6 %collective-permute-start.2 = (bf16[320,1,128]{2,1,0:T(2,128)(2,1)S(1)}, bf16[320,1,128]{2,1,0:T(2,128)(2,1)S(1)}, u32[]{:S(2)}, u32[]{:S(2)}) collective-permute-start(bf16[320,1,128]{2,1,0:T(2,128)(2,1)S(1)} %get-tuple-element.17), channel_id=1, source_target_pairs={{0,1},{2,3},{4,5},{6,7},{8,9},{10,11},{12,13},{14,15},{16,17},{18,... | collective-permute-start | bytes 245768 | tf_op jit(solution)/shard_map/ppermute | solution.py:19
  33.8 1.3 collective-permute-start.3
  35.1 1.5 collective-permute-done.2
  36.6 4.4 %collective-permute-done.3 = bf16[320,1,128]{2,1,0:T(2,128)(2,1)S(1)} collective-permute-done((bf16[320,1,128]{2,1,0:T(2,128)(2,1)S(1)}, bf16[320,1,128]{2,1,0:T(2,128)(2,1)S(1)}, u32[]{:S(2)}, u32[]{:S(2)}) %collective-permute-start.3) | collective-permute-done | bytes 81952 | tf_op jit(solution)/shard_map/ppermute | solution.py:21
  41.0 2.7 fusion.6
  43.7 1.3 fusion.146
  45.8 0.6 pad_maximum_fusion
  46.5 0.5 convolution_add_fusion.16
  47.8 0.5 convolution_add_fusion.14
  48.3 0.5 convolution_add_fusion.13
  49.8 0.5 convolution_add_fusion.10
  50.4 0.5 fusion.13
  50.9 0.8 copy-done.1
  51.8 1.3 convolution_convert_fusion.2
  53.1 0.9 convert_element_type.100
  54.0 23.7 %all-gather = bf16[512,640]{1,0:T(8,128)(2,1)S(1)} all-gather(bf16[32,640]{1,0:T(8,128)(2,1)S(1)} %convert_element_type.100), channel_id=2, replica_groups=mesh['img'=16,'row'=2] {'img'}, dimensions={0}, use_global_device_ids=true | all-gather | bytes 696320 | tf_op jit(solution)/shard_map/all_gather | solution.py:190
  77.9 4.7 %all_gather.13 = bf16[64,640]{1,0:T(8,128)(2,1)S(1)} all-gather(bf16[32,640]{1,0:T(8,128)(2,1)S(1)} %fusion.15), channel_id=1, replica_groups=mesh['img'=16,'row'=2] {'row'}, dimensions={0}, use_global_device_ids=true | all-gather | bytes 122880 | tf_op jit(solution)/shard_map/all_gather | solution.py:195
  82.6 0.6 fusion.148
  83.2 0.9 copy.37
  84.1 0.8 copy.26
  84.9 2.7 fusion.150
  87.6 2.0 multiply_reduce_fusion
  90.4 0.6 copy-done.25
  91.2 0.5 fusion.11
  91.8 1.3 fusion.151
  93.1 1.2 convolution_convert_fusion.5
  94.7 0.7 copy-done.30
  95.7 0.7 copy-done.20
  96.5 1.3 fusion.29
  97.8 1.3 fusion.28
  99.1 1.3 fusion.27
  100.5 1.3 fusion.26
  101.8 1.3 fusion.25
  103.1 1.3 fusion.24
  104.4 1.3 fusion.23
  105.7 1.4 fusion.22
  107.1 1.4 fusion.21
  108.4 0.7 pad_maximum_fusion.2
  109.1 1.7 copy.35
  110.9 2.6 convolution_bitcast_fusion.1
  113.6 0.6 dynamic_slice.8
  114.1 0.6 iota_compare_fusion.5
  114.8 2.1 reduce-scatter.7.cloned.1.call-done
  116.9 24.5 %all-gather.1 = bf16[512,640]{1,0:T(8,128)(2,1)S(1)} all-gather(bf16[32,640]{1,0:T(8,128)(2,1)} %reduce-scatter.7.cloned.1.call-done), channel_id=3, replica_groups=mesh['img'=16,'row'=2] {'img'}, dimensions={0}, use_global_device_ids=true | all-gather | bytes 696320 | tf_op jit(solution)/shard_map/all_gather | solution.py:203
  141.6 5.1 %all_gather.15 = bf16[64,640]{1,0:T(8,128)(2,1)S(1)} all-gather(bf16[32,640]{1,0:T(8,128)(2,1)S(1)} %fusion.14), channel_id=1, replica_groups=mesh['img'=16,'row'=2] {'row'}, dimensions={0}, use_global_device_ids=true | all-gather | bytes 122880 | tf_op jit(solution)/shard_map/all_gather | solution.py:209
  146.8 3.4 convolution_convert_fusion
  150.1 1.9 fusion.20
  152.0 1.0 copy.56
  153.0 4.5 %convolution_convert_fusion.1 = bf16[64,3328]{1,0:T(8,128)(2,1)} fusion(bf16[64,640]{1,0:T(8,128)(2,1)S(1)} %all_gather.15, bf16[3328,640]{1,0:T(8,128)(2,1)} %param.18), kind=kOutput, calls=%fused_computation.6 | convolution fusion | flops 272842752 | bytes 4767744 | tf_op jit(solution)/shard_map/dot_general | solution.py:210
  157.5 2.0 broadcast_in_dim.43
  159.4 3.1 dynamic_update_slice.3
  162.5 110.7 %all-reduce.9.cloned.1.call-done = (f32[3,3,320,320]{3,2,1,0:T(8,128)}, f32[320,320]{1,0:T(8,128)}, f32[320,320]{1,0:T(8,128)}) async-done(((f32[3,3,320,320]{3,2,1,0:T(8,128)}, f32[320,320]{1,0:T(8,128)}, f32[320,320]{1,0:T(8,128)}), (f32[3,3,320,320]{3,2,1,0:T(8,128)}, f32[320,320]{1,0:T(8,128)}, f32[320,320]{1,0:T(8,128)})) %all-reduce.9.cloned.1.call-update) | async-done | bytes 4505616 | tf_op jit(solution)/shard_map/psum | solution.py:226
  273.2 1.8 multiply_convert_fusion.3
  274.9 1.8 multiply_convert_fusion.4
  276.7 4.1 %multiply_convert_fusion.1 = bf16[3,3,320,320]{3,2,1,0:T(8,128)(2,1)} fusion(f32[3,3,320,320]{3,2,1,0:T(8,128)} %get-tuple-element.6), kind=kLoop, calls=%fused_computation.7 | loop fusion | flops 1843200 | bytes 5529600 | tf_op jit(solution)/shard_map/convert_element_type | solution.py:227
  280.8 107.4 %all-reduce.7.cloned.1.call-done = bf16[3328,640]{1,0:T(8,128)(2,1)} async-done(((bf16[3328,640]{1,0:T(8,128)(2,1)}), bf16[3328,640]{1,0:T(8,128)(2,1)}) %all-reduce.7.cloned.1.call-update) | async-done | bytes 4259856 | tf_op jit(solution)/shard_map/psum | solution.py:219
  388.1 5.0 %multiply_convert_fusion = bf16[3328,640]{1,0:T(8,128)(2,1)} fusion(bf16[3328,640]{1,0:T(8,128)(2,1)} %all-reduce.7.cloned.1.call-done), kind=kLoop, calls=%fused_computation.1 | loop fusion | flops 6389760 | bytes 8519680 | tf_op jit(solution)/shard_map/convert_element_type | solution.py:220
  (104 shorter events, 9.2 us)
Async XLA Ops:
  7.2 11.3 %copy-start = (bf16[512,3328]{1,0:T(8,128)(2,1)S(1)}, bf16[512,3328]{1,0:T(8,128)(2,1)}, u32[]{:S(2)}) copy-start(bf16[512,3328]{1,0:T(8,128)(2,1)} %param.12) | copy-start | bytes 10223620
  7.2 45.9 %reduce-scatter.5.cloned.1.call-start = ((), (), s32[]{:S(2)}) async-start(), calls=%async_computation.2 | async-start | bytes 245760 | tf_op jit(solution)/shard_map/reduce_scatter | solution.py:185
  11.6 13.4 %collective-permute-start = (bf16[4,1,128]{2,1,0:T(2,128)(2,1)S(1)}, bf16[4,1,128]{2,1,0:T(2,128)(2,1)S(1)}, u32[]{:S(2)}, u32[]{:S(2)}) collective-permute-start(bf16[4,1,128]{2,1,0:T(2,128)(2,1)S(1)} %get-tuple-element.29), channel_id=1, source_target_pairs={{0,1},{2,3},{4,5},{6,7},{8,9},{10,11},{12,13},{14,15},{16,17},{18,... | collective-permute-start | bytes 3080 | tf_op jit(solution)/shard_map/ppermute | solution.py:19
  16.5 8.5 %collective-permute-start.1 = (bf16[4,1,128]{2,1,0:T(2,128)(2,1)S(1)}, bf16[4,1,128]{2,1,0:T(2,128)(2,1)S(1)}, u32[]{:S(2)}, u32[]{:S(2)}) collective-permute-start(bf16[4,1,128]{2,1,0:T(2,128)(2,1)S(1)} %get-tuple-element.30), channel_id=1, source_target_pairs={{1,0},{3,2},{5,4},{7,6},{9,8},{11,10},{13,12},{15,14},{17,16},{19,... | collective-permute-start | bytes 3080 | tf_op jit(solution)/shard_map/ppermute | solution.py:21
  22.2 3.0 copy-start.27
  22.2 94.7 %reduce-scatter.7.cloned.1.call-start = ((), (), s32[]{:S(2)}) async-start(), calls=%async_computation.4 | async-start | bytes 122880 | tf_op jit(solution)/shard_map/reduce_scatter | solution.py:200
  28.8 19.5 %copy-start.3 = (bf16[320,1024]{1,0:T(8,128)(2,1)}, bf16[320,1024]{1,0:T(8,128)(2,1)S(1)}, u32[]{:S(2)}) copy-start(bf16[320,1024]{1,0:T(8,128)(2,1)S(1)} %get-tuple-element.31) | copy-start | bytes 1966084
  28.8 6.2 %copy-start.29 = (s32[16]{0:T(128)S(1)}, s32[16]{0:T(128)}, u32[]{:S(2)}) copy-start(s32[16]{0:T(128)} %param.14) | copy-start | bytes 196
  29.2 7.4 %collective-permute-start.2 = (bf16[320,1,128]{2,1,0:T(2,128)(2,1)S(1)}, bf16[320,1,128]{2,1,0:T(2,128)(2,1)S(1)}, u32[]{:S(2)}, u32[]{:S(2)}) collective-permute-start(bf16[320,1,128]{2,1,0:T(2,128)(2,1)S(1)} %get-tuple-element.17), channel_id=1, source_target_pairs={{0,1},{2,3},{4,5},{6,7},{8,9},{10,11},{12,13},{14,15},{16,17},{18,... | collective-permute-start | bytes 245768 | tf_op jit(solution)/shard_map/ppermute | solution.py:19
  33.8 7.2 %collective-permute-start.3 = (bf16[320,1,128]{2,1,0:T(2,128)(2,1)S(1)}, bf16[320,1,128]{2,1,0:T(2,128)(2,1)S(1)}, u32[]{:S(2)}, u32[]{:S(2)}) collective-permute-start(bf16[320,1,128]{2,1,0:T(2,128)(2,1)S(1)} %get-tuple-element.18), channel_id=1, source_target_pairs={{1,0},{3,2},{5,4},{7,6},{9,8},{11,10},{13,12},{15,14},{17,16},{19,... | collective-permute-start | bytes 245768 | tf_op jit(solution)/shard_map/ppermute | solution.py:21
  43.7 1.6 copy-start.23
  45.0 1.4 copy-start.19
  45.0 2.2 copy-start.17
  45.0 2.7 copy-start.15
  45.1 3.8 copy-start.13
  45.1 4.3 %copy-start.11 = (bf16[320,8,128]{2,1,0:T(8,128)(2,1)}, bf16[320,8,128]{2,1,0:T(8,128)(2,1)S(1)}, u32[]{:S(2)}) copy-start(bf16[320,8,128]{2,1,0:T(8,128)(2,1)S(1)} %get-tuple-element.10) | copy-start | bytes 1966084
  45.1 5.3 %copy-start.21 = (bf16[320,8,128]{2,1,0:T(8,128)(2,1)}, bf16[320,8,128]{2,1,0:T(8,128)(2,1)S(1)}, u32[]{:S(2)}) copy-start(bf16[320,8,128]{2,1,0:T(8,128)(2,1)S(1)} %get-tuple-element.9) | copy-start | bytes 1966084
  46.4 0.8 copy-start.9
  46.5 3.4 copy-start.7
  50.4 1.4 copy-start.24
  50.9 0.8 copy-start.1
  87.6 2.1 copy-start.6
  90.0 0.9 copy-start.25
  90.0 1.2 copy-start.28
  90.3 1.4 copy-start.2
  91.8 1.3 copy-start.26
  93.1 1.2 copy-start.5
  94.3 1.1 copy-start.30
  95.4 1.1 copy-start.20
  96.5 1.3 copy-start.10
  97.8 1.3 copy-start.18
  99.1 1.3 copy-start.16
  100.5 1.3 copy-start.4
  101.8 1.3 copy-start.14
  103.1 1.3 copy-start.12
  104.4 1.3 copy-start.8
  105.7 1.4 copy-start.22
  110.8 162.3 %all-reduce.9.cloned.1.call-start = ((), (), s32[]{:S(2)}) async-start(), calls=%async_computation.5 | async-start | bytes 10813440 | tf_op jit(solution)/shard_map/psum | solution.py:226
  113.5 274.6 %all-reduce.7.cloned.1.call-start = ((), (), s32[]{:S(2)}) async-start(), calls=%async_computation.3 | async-start | bytes 8519680 | tf_op jit(solution)/shard_map/psum | solution.py:219
Sparse Core Ops, SparseCore 0:
  22.3 13.0 reduce-scatter.4
  111.0 5.9 reduce-scatter.6
  123.0 150.1 all-reduce.8
  277.3 110.8 all-reduce.6
where the time goes:
time: 401 us; the launch traced here: 400 us
  waiting for transfers between devices  226 us (56%)
  blocking collectives  58 us (14%)
  matrix products  48.8 us (12%)
  other arithmetic  21 us (5%)
  between operations  17.3 us (4%)
  local copies, waits for them, and re-layouts  16.3 us (4%)
  starting transfers between devices  12.2 us (3%)
    psum x1, waiting for transfers between devices, shards(): lax.psum((res_grad, query_grad, out_grad), ('img', 'row'))  111 us
    psum x1, waiting for transfers between devices, shards(): lax.psum(kv_weight_part.astype(jnp.bfloat16), 'img').astype(jnp.float32)  107 us
    all_gather x1, blocking collectives, shards(): shard_piece = lax.all_gather(grad_band[None], 'img', axis=0, tiled=True)  24.5 us
    all_gather x1, blocking collectives, shards(): lax.all_gather(kv_band[None], 'img', axis=0, tiled=True).astype(jnp.float32)  23.7 us
    dot_general x9, matrix products, filter_grad(): lax.dot_general(upstream, window, (((1,), (1,)), ((), ())), preferred_ele...  11.9 us
    ppermute x2, starting transfers between devices, extended(): lax.ppermute(tail, axis, [(i, (i + 1) % count) for i in range(ends)])  9.45 us
    dot_general x18, matrix products, convolve(): jnp.dot(weight[row_tap, col_tap], window, preferred_element_type=jnp.floa...  8.1 us
  transfers between devices with their start and end apart: 8, of which 5 were waited for; matrix products, arithmetic and copies ran while one was open for 12% of the time, Pallas kernels for 0%

commit v1 on v0

--- a/solution.py
+++ b/solution.py
@@ -223,7 +223,10 @@
     weight_scale = (
         lax.axis_size("img") * lax.axis_size("row") * latents.shape[2] * latents.shape[3]
     ) ** (-0.5)
-    res_total, query_total, out_total = lax.psum((res_grad, query_grad, out_grad), ("img", "row"))
+    _start_layers_all = lambda q_in: jax.lax.psum(
+        jax.lax.psum(q_in, axis_name="row"), axis_name="img"
+    )
+    res_total, query_total, out_total = _start_layers_all((res_grad, query_grad, out_grad))
     grad_res_weight = (res_total * weight_scale).astype(jnp.bfloat16)
     grad_query_weight = (query_total * weight_scale).astype(jnp.bfloat16)
     grad_out_weight = (out_total * weight_scale).astype(jnp.bfloat16)

time: 401 us -> 514 us (1.28)
  waiting for transfers between devices: 226 us -> 342 us
    psum x1 -> x2, waiting for transfers between devices: 111 us -> 230 us  [the longest x1 125 us: shards(): jax.lax.psum(jax.lax.psum(q_in, axis_name='row'), axis_name='img')]
  transfers between devices with their start and end apart: 8 -> 9, of which waited for: 5 -> 6; matrix products, arithmetic and copies ran while one was open for 12% -> 9% of each run, Pallas kernels for 0% -> 0%
where the time goes in v1:
time: 514 us; the launch traced here: 513 us
  waiting for transfers between devices  342 us (67%)
  blocking collectives  57.6 us (11%)
  matrix products  48.6 us (9%)
  other arithmetic  19.1 us (4%)
  between operations  17.3 us (3%)
  local copies, waits for them, and re-layouts  16.3 us (3%)
  starting transfers between devices  12.5 us (2%)
    psum x1, waiting for transfers between devices, shards(): jax.lax.psum(jax.lax.psum(q_in, axis_name='row'), axis_name='img')  125 us
    psum x1, waiting for transfers between devices, shards(): jax.lax.psum(q_in, axis_name='row')  105 us
    psum x1, waiting for transfers between devices, shards(): lax.psum(kv_weight_part.astype(jnp.bfloat16), 'img').astype(jnp.float32)  104 us
    all_gather x1, blocking collectives, shards(): lax.all_gather(kv_band[None], 'img', axis=0, tiled=True).astype(jnp.float32)  23.6 us
    all_gather x1, blocking collectives, shards(): shard_piece = lax.all_gather(grad_band[None], 'img', axis=0, tiled=True)  23.5 us
    dot_general x9, matrix products, filter_grad(): lax.dot_general(upstream, window, (((1,), (1,)), ((), ())), preferred_ele...  12 us
  transfers between devices with their start and end apart: 9, of which 6 were waited for; matrix products, arithmetic and copies ran while one was open for 9% of the time, Pallas kernels for 0%

profile of v1, /device:TPU:0, one launch (start us, length us, event | category | flops | bytes accessed | tf_op | source)
XLA Modules:
  0.0 513.2 jit_solution(4509876904242219122)
XLA Ops:
  8.8 0.6 select_reduce_fusion
  10.8 0.7 add_convert_fusion
  11.6 4.9 collective-permute-start
  16.5 1.3 collective-permute-start.1
  18.5 3.7 fusion.68
  22.3 2.6 convolution_convert_fusion.4
  28.2 0.6 fusion.19
  29.2 4.6 collective-permute-start.2
  33.8 1.3 collective-permute-start.3
  35.1 1.5 collective-permute-done.2
  36.6 4.4 collective-permute-done.3
  41.0 2.7 fusion.6
  43.7 1.3 fusion.146
  45.8 0.6 pad_maximum_fusion
  46.5 0.5 convolution_add_fusion.16
  47.8 0.5 convolution_add_fusion.14
  49.8 0.5 convolution_add_fusion.10
  50.4 0.5 fusion.13
  50.9 0.8 copy-done.1
  51.8 1.3 convolution_convert_fusion.2
  53.1 0.9 convert_element_type.100
  54.0 23.6 %all-gather = bf16[512,640]{1,0:T(8,128)(2,1)S(1)} all-gather(bf16[32,640]{1,0:T(8,128)(2,1)S(1)} %convert_element_type.100), channel_id=2, replica_groups=mesh['img'=16,'row'=2] {'img'}, dimensions={0}, use_global_device_ids=true | all-gather | bytes 696320 | tf_op jit(solution)/shard_map/all_gather | solution.py:190
  77.8 4.7 all_gather.13
  82.5 0.6 fusion.148
  83.1 0.9 copy.37
  84.0 0.8 copy.26
  84.8 2.7 fusion.150
  87.5 2.0 multiply_reduce_fusion
  90.3 0.6 copy-done.27
  91.2 0.5 fusion.11
  91.7 1.3 fusion.151
  93.1 1.2 convolution_convert_fusion.5
  94.6 0.7 copy-done.32
  95.7 0.7 copy-done.20
  96.4 1.3 fusion.29
  97.7 1.3 fusion.28
  99.1 1.3 fusion.27
  100.4 1.3 fusion.26
  101.7 1.3 fusion.25
  103.1 1.3 fusion.24
  104.4 1.3 fusion.23
  105.7 1.4 fusion.22
  107.0 1.4 fusion.21
  108.4 0.7 pad_maximum_fusion.2
  109.1 1.7 copy.35
  110.8 2.6 convolution_bitcast_fusion.1
  113.5 0.6 dynamic_slice.8
  114.1 0.6 iota_compare_fusion.5
  114.8 2.1 reduce-scatter.7.cloned.1.call-done
  116.9 23.5 %all-gather.1 = bf16[512,640]{1,0:T(8,128)(2,1)S(1)} all-gather(bf16[32,640]{1,0:T(8,128)(2,1)} %reduce-scatter.7.cloned.1.call-done), channel_id=3, replica_groups=mesh['img'=16,'row'=2] {'img'}, dimensions={0}, use_global_device_ids=true | all-gather | bytes 696320 | tf_op jit(solution)/shard_map/all_gather | solution.py:203
  140.5 5.8 %all_gather.15 = bf16[64,640]{1,0:T(8,128)(2,1)S(1)} all-gather(bf16[32,640]{1,0:T(8,128)(2,1)S(1)} %fusion.14), channel_id=1, replica_groups=mesh['img'=16,'row'=2] {'row'}, dimensions={0}, use_global_device_ids=true | all-gather | bytes 122880 | tf_op jit(solution)/shard_map/all_gather | solution.py:209
  146.4 3.4 convolution_convert_fusion
  150.0 105.1 %all-reduce.13.cloned.1.call-done = (f32[3,3,320,320]{3,2,1,0:T(8,128)}, f32[320,320]{1,0:T(8,128)}, f32[320,320]{1,0:T(8,128)}) async-done(((f32[3,3,320,320]{3,2,1,0:T(8,128)}, f32[320,320]{1,0:T(8,128)}, f32[320,320]{1,0:T(8,128)}), (f32[3,3,320,320]{3,2,1,0:T(8,128)}, f32[320,320]{1,0:T(8,128)}, f32[320,320]{1,0:T(8,128)})) %all-reduce.13.cloned.1.call-update) | async-done | bytes 4505616 | tf_op jit(solution)/shard_map/psum | solution.py:227
  255.2 1.9 fusion.20
  257.0 1.0 copy.56
  258.0 4.3 convolution_convert_fusion.1
  262.3 2.0 broadcast_in_dim.43
  264.3 3.1 dynamic_update_slice.3
  267.4 103.7 %all-reduce.9.cloned.1.call-done = bf16[3328,640]{1,0:T(8,128)(2,1)} async-done(((bf16[3328,640]{1,0:T(8,128)(2,1)}), bf16[3328,640]{1,0:T(8,128)(2,1)}) %all-reduce.9.cloned.1.call-update) | async-done | bytes 4259856 | tf_op jit(solution)/shard_map/psum | solution.py:219
  371.1 5.0 multiply_convert_fusion
  376.1 124.9 %all-reduce.11.cloned.1.call-done = (f32[3,3,320,320]{3,2,1,0:T(8,128)}, f32[320,320]{1,0:T(8,128)}, f32[320,320]{1,0:T(8,128)}) async-done(((f32[3,3,320,320]{3,2,1,0:T(8,128)}, f32[320,320]{1,0:T(8,128)}, f32[320,320]{1,0:T(8,128)}), (f32[3,3,320,320]{3,2,1,0:T(8,128)}, f32[320,320]{1,0:T(8,128)}, f32[320,320]{1,0:T(8,128)})) %all-reduce.11.cloned.1.call-update) | async-done | bytes 4505616 | tf_op jit(solution)/shard_map/psum | solution.py:226
  501.0 4.2 multiply_convert_fusion.1
  505.2 0.7 multiply_convert_fusion.3
  505.9 0.7 multiply_convert_fusion.4
  (111 shorter events, 10.0 us)
Async XLA Ops:
  7.2 11.3 %copy-start = (bf16[512,3328]{1,0:T(8,128)(2,1)S(1)}, bf16[512,3328]{1,0:T(8,128)(2,1)}, u32[]{:S(2)}) copy-start(bf16[512,3328]{1,0:T(8,128)(2,1)} %param.12) | copy-start | bytes 10223620
  7.2 45.9 %reduce-scatter.5.cloned.1.call-start = ((), (), s32[]{:S(2)}) async-start(), calls=%async_computation.2 | async-start | bytes 245760 | tf_op jit(solution)/shard_map/reduce_scatter | solution.py:185
  11.6 13.4 %collective-permute-start = (bf16[4,1,128]{2,1,0:T(2,128)(2,1)S(1)}, bf16[4,1,128]{2,1,0:T(2,128)(2,1)S(1)}, u32[]{:S(2)}, u32[]{:S(2)}) collective-permute-start(bf16[4,1,128]{2,1,0:T(2,128)(2,1)S(1)} %get-tuple-element.32), channel_id=1, source_target_pairs={{0,1},{2,3},{4,5},{6,7},{8,9},{10,11},{12,13},{14,15},{16,17},{18,... | collective-permute-start | bytes 3080 | tf_op jit(solution)/shard_map/ppermute | solution.py:19
  16.5 8.5 %collective-permute-start.1 = (bf16[4,1,128]{2,1,0:T(2,128)(2,1)S(1)}, bf16[4,1,128]{2,1,0:T(2,128)(2,1)S(1)}, u32[]{:S(2)}, u32[]{:S(2)}) collective-permute-start(bf16[4,1,128]{2,1,0:T(2,128)(2,1)S(1)} %get-tuple-element.33), channel_id=1, source_target_pairs={{1,0},{3,2},{5,4},{7,6},{9,8},{11,10},{13,12},{15,14},{17,16},{19,... | collective-permute-start | bytes 3080 | tf_op jit(solution)/shard_map/ppermute | solution.py:21
  22.2 3.0 copy-start.29
  22.2 94.7 %reduce-scatter.7.cloned.1.call-start = ((), (), s32[]{:S(2)}) async-start(), calls=%async_computation.4 | async-start | bytes 122880 | tf_op jit(solution)/shard_map/reduce_scatter | solution.py:200
  28.8 19.5 %copy-start.3 = (bf16[320,1024]{1,0:T(8,128)(2,1)}, bf16[320,1024]{1,0:T(8,128)(2,1)S(1)}, u32[]{:S(2)}) copy-start(bf16[320,1024]{1,0:T(8,128)(2,1)S(1)} %get-tuple-element.34) | copy-start | bytes 1966084
  28.8 6.2 %copy-start.31 = (s32[16]{0:T(128)S(1)}, s32[16]{0:T(128)}, u32[]{:S(2)}) copy-start(s32[16]{0:T(128)} %param.14) | copy-start | bytes 196
  29.2 7.4 %collective-permute-start.2 = (bf16[320,1,128]{2,1,0:T(2,128)(2,1)S(1)}, bf16[320,1,128]{2,1,0:T(2,128)(2,1)S(1)}, u32[]{:S(2)}, u32[]{:S(2)}) collective-permute-start(bf16[320,1,128]{2,1,0:T(2,128)(2,1)S(1)} %get-tuple-element.20), channel_id=1, source_target_pairs={{0,1},{2,3},{4,5},{6,7},{8,9},{10,11},{12,13},{14,15},{16,17},{18,... | collective-permute-start | bytes 245768 | tf_op jit(solution)/shard_map/ppermute | solution.py:19
  33.8 7.2 %collective-permute-start.3 = (bf16[320,1,128]{2,1,0:T(2,128)(2,1)S(1)}, bf16[320,1,128]{2,1,0:T(2,128)(2,1)S(1)}, u32[]{:S(2)}, u32[]{:S(2)}) collective-permute-start(bf16[320,1,128]{2,1,0:T(2,128)(2,1)S(1)} %get-tuple-element.21), channel_id=1, source_target_pairs={{1,0},{3,2},{5,4},{7,6},{9,8},{11,10},{13,12},{15,14},{17,16},{19,... | collective-permute-start | bytes 245768 | tf_op jit(solution)/shard_map/ppermute | solution.py:21
  43.7 1.6 copy-start.23
  45.0 1.4 copy-start.19
  45.0 2.2 copy-start.17
  45.0 2.7 copy-start.15
  45.1 3.8 copy-start.13
  45.1 4.3 copy-start.11
  45.1 5.3 %copy-start.21 = (bf16[320,8,128]{2,1,0:T(8,128)(2,1)}, bf16[320,8,128]{2,1,0:T(8,128)(2,1)S(1)}, u32[]{:S(2)}) copy-start(bf16[320,8,128]{2,1,0:T(8,128)(2,1)S(1)} %get-tuple-element.12) | copy-start | bytes 1966084
  46.4 0.8 copy-start.9
  46.5 3.4 copy-start.7
  50.4 1.4 copy-start.26
  50.9 0.8 copy-start.1
  87.5 2.1 copy-start.6
  89.9 0.9 copy-start.27
  90.0 1.2 copy-start.30
  90.3 1.4 copy-start.2
  91.7 1.3 copy-start.28
  93.1 1.2 copy-start.5
  94.2 1.1 copy-start.32
  95.3 1.1 copy-start.20
  96.4 1.3 copy-start.10
  97.7 1.3 copy-start.18
  99.1 1.3 copy-start.16
  100.4 1.3 copy-start.4
  101.7 1.3 copy-start.14
  103.1 1.3 copy-start.12
  104.4 1.3 copy-start.8
  105.7 1.4 copy-start.22
  110.8 144.3 %all-reduce.13.cloned.1.call-start = ((), (), s32[]{:S(2)}) async-start(), calls=%async_computation.6 | async-start | bytes 10813440 | tf_op jit(solution)/shard_map/psum | solution.py:227
  113.5 257.6 %all-reduce.9.cloned.1.call-start = ((), (), s32[]{:S(2)}) async-start(), calls=%async_computation.3 | async-start | bytes 8519680 | tf_op jit(solution)/shard_map/psum | solution.py:219
  149.7 351.3 %all-reduce.11.cloned.1.call-start = ((), (), s32[]{:S(2)}) async-start(), calls=%async_computation.5 | async-start | bytes 10813440 | tf_op jit(solution)/shard_map/psum | solution.py:226
  501.0 4.2 copy-start.25
  501.0 4.9 copy-start.24
Sparse Core Ops, SparseCore 0:
  22.3 13.0 reduce-scatter.4
  110.9 5.9 reduce-scatter.6
  120.1 135.0 all-reduce.12
  259.2 111.7 all-reduce.8
  374.9 126.0 all-reduce.10
